TPU v7x, 512 devices: a whole 4x4x16 slice. The times are simulated.
512 devices in a mesh: panel: 8 (over x, core), leaf: 64 (over y, z).
Axes of the slice: x: 4, y: 4, z: 16, core: 2. Of those that a mesh axis runs over, the one named last changes fastest.
Arguments:
- sources: bfloat16 [8, 3328, 2, 1536], P('panel', 'leaf'), may hold values from -6 to 6
- transmission: float32 [8, 3328, 128], P('panel', 'leaf')
- media: int32 [8, 3328, 1], P('panel', 'leaf'), may hold values from 0 to 63; in each aligned block of 52 rows (0 to 51, 52 to 103, ..., all dimensions but the last counted through in order) at most 2 rows name the same one
- sep_code: int32 [8, 64], P('panel', 'leaf'), may hold values from 0 to 7
- leaf_factors: bfloat16 [64, 2, 768, 768], P('leaf'), may hold values from -0.15625 to 0.15625
- sep_factors: bfloat16 [2, 2, 384, 384], replicated, may hold values from -0.15625 to 0.15625
Outputs:
- solutions: bfloat16 [8, 3328, 2, 1536], P('panel', 'leaf')
Inputs may be any that keep to these rules, and one draw needn't show every extreme that they name: `media`: among the 52 leaves of one device (aligned blocks of rows) no library entry is named more than 2 times, a bound that some block reaches.
All inputs are finite; a program needn't handle non-finite values.
Results may differ from a plain program's by a relative error of at most 0.0065.
Values may be sent and summed in bfloat16 or wider, within the bound.
A program may use at most 64 MiB of HBM per device.

v0:
```python
import math

import jax
import jax.numpy as jnp
from jax import lax
from jax.sharding import PartitionSpec as P


def from_behind(value, axis, steps):
    count = lax.axis_size(axis)
    initial, last = (max(0, -steps), min(count, count - steps))
    return lax.ppermute(value, axis, [(source, source + steps) for source in range(initial, last)])


def from_partner(value, axis, distance):
    mask = 2**distance
    pairs = [(source, source ^ mask) for source in range(lax.axis_size(axis))]
    return lax.ppermute(value, axis, pairs)


def complex_times(left, right, half):
    left_re, left_im = (left[..., :half], left[..., half:])
    right_re, right_im = (right[..., :half], right[..., half:])
    return jnp.concatenate(
        [left_re * right_re - left_im * right_im, left_re * right_im + left_im * right_re], axis=-1
    )


def block_matrix(pair):
    real_part, imag_part = (pair[0], pair[1])
    upper = jnp.concatenate([real_part, imag_part], axis=1)
    lower = jnp.concatenate([-imag_part, real_part], axis=1)
    return jnp.concatenate([upper, lower], axis=0)


def face_rows(source, width, front):
    return jnp.concatenate(
        [source[..., width - front : width], source[..., 2 * width - front :]], axis=-1
    )


def lift_face(incoming, width, front):
    gap = jnp.zeros(incoming.shape[:-1] + (width - front,), jnp.float32)
    return jnp.concatenate([gap, incoming[..., :front], gap, incoming[..., front:]], axis=-1)


def lift_top(values, width, sep):
    gap = jnp.zeros(values.shape[:-1] + (width - sep,), jnp.float32)
    return jnp.concatenate([values[..., :sep], gap, values[..., sep:], gap], axis=-1)


def trace_rows(solved, width, sep):
    return jnp.concatenate([solved[..., :sep], solved[..., width : width + sep]], axis=-1)


def on_device(sources, transmission, media, sep_code, leaf_factors, sep_factors):
    leaves, shots, width2 = (sources.shape[1], sources.shape[2], sources.shape[3])
    leaf_n = width2 // 2
    front = transmission.shape[2] // 2
    sep_n = sep_factors.shape[2]
    sep_lib = sep_factors.shape[0]
    nleaf = lax.axis_size("leaf")
    levels = nleaf.bit_length() - 1
    capacity = max(2, leaves * 5 // (nleaf * 2))
    source = sources[0]
    tau = transmission[0]
    face = face_rows(source, leaf_n, front).astype(jnp.float32)

    def advance(step, incoming):
        leaving = complex_times(tau[:, None, :], incoming + face, front)
        return from_behind(leaving, "panel", 1)

    arriving = lax.fori_loop(
        0, lax.axis_size("panel") - 1, advance, jnp.zeros(face.shape, jnp.float32)
    )
    rhs = (source.astype(jnp.float32) + lift_face(arriving, leaf_n, front)).astype(jnp.bfloat16)
    kinds = media[0, :, 0]
    hits = (kinds[:, None] == jnp.arange(nleaf, dtype=jnp.int32)[None, :]).astype(jnp.int32)
    rank = jnp.sum((jnp.cumsum(hits, axis=0) - hits) * hits, axis=1)
    slot = kinds * capacity + rank
    send = jnp.zeros((nleaf * capacity, shots, width2), jnp.bfloat16).at[slot].set(rhs)
    send = send.reshape(nleaf, capacity, shots, width2)
    big_leaf = block_matrix(leaf_factors[0])
    arrived = lax.all_to_all(send, "leaf", split_axis=0, concat_axis=0, tiled=True)
    solved_here = jnp.dot(arrived.reshape(-1, width2), big_leaf, preferred_element_type=jnp.float32)
    solved_here = solved_here.astype(jnp.bfloat16).reshape(arrived.shape)
    returned = lax.all_to_all(solved_here, "leaf", split_axis=0, concat_axis=0, tiled=True)
    solved = returned.reshape(nleaf * capacity, shots, width2)[slot]
    traces = trace_rows(solved, leaf_n, sep_n)
    own_trace = jnp.sum(traces.astype(jnp.float32), axis=0)
    own_code = sep_code.reshape(1)
    partial_sum, partial_code = (own_trace, own_code)
    level_sums, level_codes = ([], [])
    for bit in range(levels):
        other_sum, other_code = from_partner((partial_sum, partial_code), "leaf", bit)
        partial_sum = partial_sum + other_sum
        partial_code = partial_code + other_code
        level_sums.append(partial_sum)
        level_codes.append(partial_code[0])
    sep_sol = jnp.zeros((shots, 2 * sep_n), jnp.float32)
    for level in reversed(range(levels)):
        scaled = level_sums[level] * (1.0 / math.sqrt(leaves * 2 ** (level + 1)))
        chosen = lax.dynamic_index_in_dim(
            sep_factors, level_codes[level] % sep_lib, 0, keepdims=False
        )
        operand = (scaled - sep_sol).astype(jnp.bfloat16)
        sep_sol = jnp.dot(operand, block_matrix(chosen), preferred_element_type=jnp.float32)
    result = solved.astype(jnp.float32) - lift_top(sep_sol[None], leaf_n, sep_n)
    return result.astype(jnp.bfloat16)[None]


def solution(mesh):
    return jax.shard_map(
        on_device,
        mesh=mesh,
        in_specs=(
            P("panel", "leaf", None, None),
            P("panel", "leaf", None),
            P("panel", "leaf", None),
            P("panel", "leaf"),
            P("leaf", None, None, None),
            P(),
        ),
        out_specs=P("panel", "leaf", None, None),
        check_vma=False,
    )
```

profile of v0, /device:TPU:36, one launch (start us, length us, event | category | flops | bytes accessed | tf_op | source)
XLA Modules:
  0.0 268.3 jit_solution(256041932576104896)
XLA Ops:
  0.0 0.9 fusion.108
  0.9 0.7 copy.7
  1.8 40.9 %while.10 = (s32[]{:T(128)}, f32[52,2,128]{2,1,0:T(2,128)S(1)}, f32[1,52,128]{2,1,0:T(8,128)S(1)}, f32[52,2,128]{2,1,0:T(2,128)S(1)}, s32[]{:T(128)}) while((s32[]{:T(128)}, f32[52,2,128]{2,1,0:T(2,128)S(1)}, f32[1,52,128]{2,1,0:T(8,128)S(1)}, f32[52,2,128]{2,1,0:T(2,128)S(1)}, s32[]{:T(128)}) %tuple.51), condition=%wide.region_3.4_spmd, body=%wide.region_2.0_spmd.sunk | while | flops 66562 | bytes 665701 | solution.py:73
  1.9 0.1 multiply_subtract_fusion.2
  2.2 1.9 collective-permute-start
  4.1 3.5 %collective-permute-done = f32[52,2,128]{2,1,0:T(2,128)S(1)} collective-permute-done((f32[52,2,128]{2,1,0:T(2,128)S(1)}, f32[52,2,128]{2,1,0:T(2,128)S(1)}, u32[]{:S(2)}, u32[]{:S(2)}) %collective-permute-start) | collective-permute-done | bytes 53280 | tf_op jit(solution)/shard_map/while/body/eval_jaxpr/ppermute | solution.py:12
  7.7 0.1 multiply_subtract_fusion.2
  8.0 1.9 collective-permute-start
  9.9 3.5 %collective-permute-done = f32[52,2,128]{2,1,0:T(2,128)S(1)} collective-permute-done((f32[52,2,128]{2,1,0:T(2,128)S(1)}, f32[52,2,128]{2,1,0:T(2,128)S(1)}, u32[]{:S(2)}, u32[]{:S(2)}) %collective-permute-start) | collective-permute-done | bytes 53280 | tf_op jit(solution)/shard_map/while/body/eval_jaxpr/ppermute | solution.py:12
  13.8 1.9 collective-permute-start
  15.8 3.5 %collective-permute-done = f32[52,2,128]{2,1,0:T(2,128)S(1)} collective-permute-done((f32[52,2,128]{2,1,0:T(2,128)S(1)}, f32[52,2,128]{2,1,0:T(2,128)S(1)}, u32[]{:S(2)}, u32[]{:S(2)}) %collective-permute-start) | collective-permute-done | bytes 53280 | tf_op jit(solution)/shard_map/while/body/eval_jaxpr/ppermute | solution.py:12
  19.7 1.9 collective-permute-start
  21.6 3.5 %collective-permute-done = f32[52,2,128]{2,1,0:T(2,128)S(1)} collective-permute-done((f32[52,2,128]{2,1,0:T(2,128)S(1)}, f32[52,2,128]{2,1,0:T(2,128)S(1)}, u32[]{:S(2)}, u32[]{:S(2)}) %collective-permute-start) | collective-permute-done | bytes 53280 | tf_op jit(solution)/shard_map/while/body/eval_jaxpr/ppermute | solution.py:12
  25.5 1.9 collective-permute-start
  27.5 3.5 %collective-permute-done = f32[52,2,128]{2,1,0:T(2,128)S(1)} collective-permute-done((f32[52,2,128]{2,1,0:T(2,128)S(1)}, f32[52,2,128]{2,1,0:T(2,128)S(1)}, u32[]{:S(2)}, u32[]{:S(2)}) %collective-permute-start) | collective-permute-done | bytes 53280 | tf_op jit(solution)/shard_map/while/body/eval_jaxpr/ppermute | solution.py:12
  31.4 1.9 collective-permute-start
  33.3 3.5 %collective-permute-done = f32[52,2,128]{2,1,0:T(2,128)S(1)} collective-permute-done((f32[52,2,128]{2,1,0:T(2,128)S(1)}, f32[52,2,128]{2,1,0:T(2,128)S(1)}, u32[]{:S(2)}, u32[]{:S(2)}) %collective-permute-start) | collective-permute-done | bytes 53280 | tf_op jit(solution)/shard_map/while/body/eval_jaxpr/ppermute | solution.py:12
  37.2 1.9 collective-permute-start
  39.1 3.5 %collective-permute-done = f32[52,2,128]{2,1,0:T(2,128)S(1)} collective-permute-done((f32[52,2,128]{2,1,0:T(2,128)S(1)}, f32[52,2,128]{2,1,0:T(2,128)S(1)}, u32[]{:S(2)}, u32[]{:S(2)}) %collective-permute-start) | collective-permute-done | bytes 53280 | tf_op jit(solution)/shard_map/while/body/eval_jaxpr/ppermute | solution.py:12
  42.9 1.8 concatenate.79
  44.7 1.5 add_convert_fusion
  46.4 0.2 select_reduce_fusion
  46.6 1.3 broadcast_in_dim.19
  47.8 8.1 %scatter_fusion = bf16[128,2,1536]{2,1,0:T(2,128)(2,1)} fusion(bf16[128,2,1536]{2,1,0:T(2,128)(2,1)} %broadcast_in_dim.19, s32[52]{0:T(128)S(1)} %fusion.87, bf16[52,2,1536]{2,1,0:T(2,128)(2,1)S(1)} %add_convert_fusion), kind=kCustom, calls=%fused_computation.1 | custom fusion | bytes 958672 | tf_op jit(solution)/shard_map/scatter | solution.py:81
  55.9 18.4 %all-to-all-start = ((bf16[64,2,2,1536]{3,2,1,0:T(2,128)(2,1)}), bf16[64,2,2,1536]{3,2,1,0:T(2,128)(2,1)S(1)}, u32[]{:S(2)}, u32[]{:S(2)}) async-start(bf16[64,2,2,1536]{3,2,1,0:T(2,128)(2,1)} %bitcast.8), calls=%async_computation | async-start | bytes 1572864 | tf_op jit(solution)/shard_map/all_to_all | solution.py:84
  74.3 1.1 fusion.100
  75.4 1.6 slice_bitcast_fusion.2
  77.0 39.0 %all-to-all-done = bf16[64,2,2,1536]{3,2,1,0:T(2,128)(2,1)S(1)} async-done(((bf16[64,2,2,1536]{3,2,1,0:T(2,128)(2,1)}), bf16[64,2,2,1536]{3,2,1,0:T(2,128)(2,1)S(1)}, u32[]{:S(2)}, u32[]{:S(2)}) %all-to-all-start) | async-done | bytes 786464 | tf_op jit(solution)/shard_map/all_to_all | solution.py:84
  116.0 0.3 reshape.88
  116.3 3.7 %fusion.8 = bf16[256,1536]{1,0:T(8,128)(2,1)S(1)} fusion(bf16[256,1536]{1,0:T(8,128)(2,1)S(1)} %reshape.88, bf16[768,768]{1,0:T(8,128)(2,1)} %get-tuple-element.57, bf16[768,768]{1,0:T(8,128)(2,1)} %fusion.100, bf16[768,768]{1,0:T(8,128)(2,1)} %get-tuple-element.56), kind=kOutput, calls=%fused_computation.15 | convolution fusion | flops 1227227136 | bytes 5111808 | tf_op jit(solution)/shard_map/dot_general | solution.py:85
  120.0 1.2 reshape.89
  121.2 6.8 %all-to-all-start.1 = ((bf16[64,2,2,1536]{3,2,1,0:T(2,128)(2,1)}), bf16[64,2,2,1536]{3,2,1,0:T(2,128)(2,1)S(1)}, u32[]{:S(2)}, u32[]{:S(2)}) async-start(bf16[64,2,2,1536]{3,2,1,0:T(2,128)(2,1)} %reshape.89), calls=%async_computation.1 | async-start | bytes 1572864 | tf_op jit(solution)/shard_map/all_to_all | solution.py:87
  128.1 42.0 %all-to-all-done.1 = bf16[64,2,2,1536]{3,2,1,0:T(2,128)(2,1)S(1)} async-done(((bf16[64,2,2,1536]{3,2,1,0:T(2,128)(2,1)}), bf16[64,2,2,1536]{3,2,1,0:T(2,128)(2,1)S(1)}, u32[]{:S(2)}, u32[]{:S(2)}) %all-to-all-start.1) | async-done | bytes 786464 | tf_op jit(solution)/shard_map/all_to_all | solution.py:87
  170.1 1.2 gather_fusion
  171.5 0.2 convert_reduce_fusion
  171.6 2.5 collective-permute-start.1
  174.2 3.0 %collective-permute-done.1 = f32[2,768]{1,0:T(2,128)S(1)} collective-permute-done((f32[2,768]{1,0:T(2,128)S(1)}, f32[2,768]{1,0:T(2,128)S(1)}, u32[]{:S(2)}, u32[]{:S(2)}) %collective-permute-start.1) | collective-permute-done | bytes 6176 | tf_op jit(solution)/shard_map/ppermute | solution.py:18
  177.2 2.4 collective-permute-start.2
  179.6 4.0 %collective-permute-done.2 = f32[2,768]{1,0:T(2,128)S(1)} collective-permute-done((f32[2,768]{1,0:T(2,128)S(1)}, f32[2,768]{1,0:T(2,128)S(1)}, u32[]{:S(2)}, u32[]{:S(2)}) %collective-permute-start.2) | collective-permute-done | bytes 6176 | tf_op jit(solution)/shard_map/ppermute | solution.py:18
  183.6 2.6 collective-permute-start.3
  186.2 6.9 %collective-permute-done.3 = f32[2,768]{1,0:T(2,128)S(1)} collective-permute-done((f32[2,768]{1,0:T(2,128)S(1)}, f32[2,768]{1,0:T(2,128)S(1)}, u32[]{:S(2)}, u32[]{:S(2)}) %collective-permute-start.3) | collective-permute-done | bytes 6176 | tf_op jit(solution)/shard_map/ppermute | solution.py:18
  193.0 6.0 %collective-permute-start.4 = (f32[2,768]{1,0:T(2,128)S(1)}, f32[2,768]{1,0:T(2,128)S(1)}, u32[]{:S(2)}, u32[]{:S(2)}) collective-permute-start(f32[2,768]{1,0:T(2,128)S(1)} %add.112), channel_id=1, source_target_pairs={{0,8},{1,9},{2,10},{3,11},{4,12},{5,13},{6,14},{7,15},{8,0},{9,1},... | collective-permute-start | bytes 18440 | tf_op jit(solution)/shard_map/ppermute | solution.py:18
  199.1 2.0 collective-permute-start.7
  201.7 2.9 %collective-permute-done.7 = s32[1]{0:T(128)} collective-permute-done((s32[1]{0:T(128)}, s32[1]{0:T(128)}, u32[]{:S(2)}, u32[]{:S(2)}) %collective-permute-start.7) | collective-permute-done | bytes 36 | tf_op jit(solution)/shard_map/ppermute | solution.py:18
  205.3 4.9 %collective-permute-start.8 = (s32[1]{0:T(128)}, s32[1]{0:T(128)}, u32[]{:S(2)}, u32[]{:S(2)}) collective-permute-start(s32[1]{0:T(128)} %add.116), channel_id=1, source_target_pairs={{0,2},{1,3},{2,0},{3,1},{4,6},{5,7},{6,4},{7,5},{8,10},{9,11},{10,... | collective-permute-start | bytes 20 | tf_op jit(solution)/shard_map/ppermute | solution.py:18
  210.2 1.4 collective-permute-done.8
  212.2 5.2 %collective-permute-start.9 = (s32[1]{0:T(128)}, s32[1]{0:T(128)}, u32[]{:S(2)}, u32[]{:S(2)}) collective-permute-start(s32[1]{0:T(128)} %add.117), channel_id=1, source_target_pairs={{0,4},{1,5},{2,6},{3,7},{4,0},{5,1},{6,2},{7,3},{8,12},{9,13},{10,... | collective-permute-start | bytes 20 | tf_op jit(solution)/shard_map/ppermute | solution.py:18
  217.4 4.1 %collective-permute-done.9 = s32[1]{0:T(128)} collective-permute-done((s32[1]{0:T(128)}, s32[1]{0:T(128)}, u32[]{:S(2)}, u32[]{:S(2)}) %collective-permute-start.9) | collective-permute-done | bytes 36 | tf_op jit(solution)/shard_map/ppermute | solution.py:18
  222.2 9.8 %collective-permute-start.10 = (s32[1]{0:T(128)}, s32[1]{0:T(128)}, u32[]{:S(2)}, u32[]{:S(2)}) collective-permute-start(s32[1]{0:T(128)} %add.118), channel_id=1, source_target_pairs={{0,8},{1,9},{2,10},{3,11},{4,12},{5,13},{6,14},{7,15},{8,0},{9,1},... | collective-permute-start | bytes 20 | tf_op jit(solution)/shard_map/ppermute | solution.py:18
  231.9 4.3 %collective-permute-done.10 = s32[1]{0:T(128)} collective-permute-done((s32[1]{0:T(128)}, s32[1]{0:T(128)}, u32[]{:S(2)}, u32[]{:S(2)}) %collective-permute-start.10) | collective-permute-done | bytes 36 | tf_op jit(solution)/shard_map/ppermute | solution.py:18
  236.9 3.2 %collective-permute-start.11 = (s32[1]{0:T(128)}, s32[1]{0:T(128)}, u32[]{:S(2)}, u32[]{:S(2)}) collective-permute-start(s32[1]{0:T(128)} %add.119), channel_id=1, source_target_pairs={{0,16},{1,17},{2,18},{3,19},{4,20},{5,21},{6,22},{7,23},{8,24},{9,... | collective-permute-start | bytes 20 | tf_op jit(solution)/shard_map/ppermute | solution.py:18
  240.1 2.2 collective-permute-done.11
  243.0 3.8 %collective-permute-start.12 = (s32[1]{0:T(128)}, s32[1]{0:T(128)}, u32[]{:S(2)}, u32[]{:S(2)}) collective-permute-start(s32[1]{0:T(128)} %add.120), channel_id=1, source_target_pairs={{0,32},{1,33},{2,34},{3,35},{4,36},{5,37},{6,38},{7,39},{8,40},{9,... | collective-permute-start | bytes 20 | tf_op jit(solution)/shard_map/ppermute | solution.py:18
  246.8 3.1 %collective-permute-done.12 = s32[1]{0:T(128)} collective-permute-done((s32[1]{0:T(128)}, s32[1]{0:T(128)}, u32[]{:S(2)}, u32[]{:S(2)}) %collective-permute-start.12) | collective-permute-done | bytes 36 | tf_op jit(solution)/shard_map/ppermute | solution.py:18
  250.5 1.9 collective-permute-start.5
  252.5 1.9 fusion.101
  254.3 1.7 collective-permute-done.5
  256.1 2.6 collective-permute-start.6
  258.6 0.2 dynamic-slice_bitcast_fusion.3
  258.8 4.2 %collective-permute-done.6 = f32[2,768]{1,0:T(2,128)S(1)} collective-permute-done((f32[2,768]{1,0:T(2,128)S(1)}, f32[2,768]{1,0:T(2,128)S(1)}, u32[]{:S(2)}, u32[]{:S(2)}) %collective-permute-start.6) | collective-permute-done | bytes 6176 | tf_op jit(solution)/shard_map/ppermute | solution.py:18
  263.1 1.8 subtract_convert_fusion.3
  264.9 1.9 subtract_convert_fusion.1
  266.8 0.5 fusion.59
  267.3 1.0 fusion.62
  (58 shorter events, 3.0 us)
Async XLA Ops:
  2.2 5.5 %collective-permute-start = (f32[52,2,128]{2,1,0:T(2,128)S(1)}, f32[52,2,128]{2,1,0:T(2,128)S(1)}, u32[]{:S(2)}, u32[]{:S(2)}) collective-permute-start(f32[52,2,128]{2,1,0:T(2,128)S(1)} %pad_maximum_fusion.2), channel_id=1, source_target_pairs={{0,64},{64,128},{128,192},{192,256},{256,320},{320,384},{384,448},... | collective-permute-start | bytes 159752 | tf_op jit(solution)/shard_map/while/body/eval_jaxpr/ppermute | solution.py:12
  8.0 5.5 %collective-permute-start = (f32[52,2,128]{2,1,0:T(2,128)S(1)}, f32[52,2,128]{2,1,0:T(2,128)S(1)}, u32[]{:S(2)}, u32[]{:S(2)}) collective-permute-start(f32[52,2,128]{2,1,0:T(2,128)S(1)} %pad_maximum_fusion.2), channel_id=1, source_target_pairs={{0,64},{64,128},{128,192},{192,256},{256,320},{320,384},{384,448},... | collective-permute-start | bytes 159752 | tf_op jit(solution)/shard_map/while/body/eval_jaxpr/ppermute | solution.py:12
  13.8 5.5 %collective-permute-start = (f32[52,2,128]{2,1,0:T(2,128)S(1)}, f32[52,2,128]{2,1,0:T(2,128)S(1)}, u32[]{:S(2)}, u32[]{:S(2)}) collective-permute-start(f32[52,2,128]{2,1,0:T(2,128)S(1)} %pad_maximum_fusion.2), channel_id=1, source_target_pairs={{0,64},{64,128},{128,192},{192,256},{256,320},{320,384},{384,448},... | collective-permute-start | bytes 159752 | tf_op jit(solution)/shard_map/while/body/eval_jaxpr/ppermute | solution.py:12
  19.7 5.5 %collective-permute-start = (f32[52,2,128]{2,1,0:T(2,128)S(1)}, f32[52,2,128]{2,1,0:T(2,128)S(1)}, u32[]{:S(2)}, u32[]{:S(2)}) collective-permute-start(f32[52,2,128]{2,1,0:T(2,128)S(1)} %pad_maximum_fusion.2), channel_id=1, source_target_pairs={{0,64},{64,128},{128,192},{192,256},{256,320},{320,384},{384,448},... | collective-permute-start | bytes 159752 | tf_op jit(solution)/shard_map/while/body/eval_jaxpr/ppermute | solution.py:12
  25.5 5.5 %collective-permute-start = (f32[52,2,128]{2,1,0:T(2,128)S(1)}, f32[52,2,128]{2,1,0:T(2,128)S(1)}, u32[]{:S(2)}, u32[]{:S(2)}) collective-permute-start(f32[52,2,128]{2,1,0:T(2,128)S(1)} %pad_maximum_fusion.2), channel_id=1, source_target_pairs={{0,64},{64,128},{128,192},{192,256},{256,320},{320,384},{384,448},... | collective-permute-start | bytes 159752 | tf_op jit(solution)/shard_map/while/body/eval_jaxpr/ppermute | solution.py:12
  31.4 5.5 %collective-permute-start = (f32[52,2,128]{2,1,0:T(2,128)S(1)}, f32[52,2,128]{2,1,0:T(2,128)S(1)}, u32[]{:S(2)}, u32[]{:S(2)}) collective-permute-start(f32[52,2,128]{2,1,0:T(2,128)S(1)} %pad_maximum_fusion.2), channel_id=1, source_target_pairs={{0,64},{64,128},{128,192},{192,256},{256,320},{320,384},{384,448},... | collective-permute-start | bytes 159752 | tf_op jit(solution)/shard_map/while/body/eval_jaxpr/ppermute | solution.py:12
  37.2 5.5 %collective-permute-start = (f32[52,2,128]{2,1,0:T(2,128)S(1)}, f32[52,2,128]{2,1,0:T(2,128)S(1)}, u32[]{:S(2)}, u32[]{:S(2)}) collective-permute-start(f32[52,2,128]{2,1,0:T(2,128)S(1)} %pad_maximum_fusion.2), channel_id=1, source_target_pairs={{0,64},{64,128},{128,192},{192,256},{256,320},{320,384},{384,448},... | collective-permute-start | bytes 159752 | tf_op jit(solution)/shard_map/while/body/eval_jaxpr/ppermute | solution.py:12
  42.7 3.5 %copy-start.6 = (s32[1,52,1]{1,2,0:T(1,128)S(1)}, s32[1,52,1]{1,2,0:T(1,128)}, u32[]{:S(2)}) copy-start(s32[1,52,1]{1,2,0:T(1,128)} %param.10) | copy-start | bytes 628
  44.7 29.6 %copy-start.1 = (bf16[1,2,768,768]{3,2,1,0:T(8,128)(2,1)S(1)}, bf16[1,2,768,768]{3,2,1,0:T(8,128)(2,1)}, u32[]{:S(2)}) copy-start(bf16[1,2,768,768]{3,2,1,0:T(8,128)(2,1)} %param.12) | copy-start | bytes 7077892
  55.9 60.1 %all-to-all-start = ((bf16[64,2,2,1536]{3,2,1,0:T(2,128)(2,1)}), bf16[64,2,2,1536]{3,2,1,0:T(2,128)(2,1)S(1)}, u32[]{:S(2)}, u32[]{:S(2)}) async-start(bf16[64,2,2,1536]{3,2,1,0:T(2,128)(2,1)} %bitcast.8), calls=%async_computation | async-start | bytes 1572864 | tf_op jit(solution)/shard_map/all_to_all | solution.py:84
  120.0 132.4 %copy-start = (bf16[2,2,384,384]{3,2,1,0:T(8,128)(2,1)S(1)}, bf16[2,2,384,384]{3,2,1,0:T(8,128)(2,1)}, u32[]{:S(2)}) copy-start(bf16[2,2,384,384]{3,2,1,0:T(8,128)(2,1)} %param.13) | copy-start | bytes 3538948
  121.2 48.9 %all-to-all-start.1 = ((bf16[64,2,2,1536]{3,2,1,0:T(2,128)(2,1)}), bf16[64,2,2,1536]{3,2,1,0:T(2,128)(2,1)S(1)}, u32[]{:S(2)}, u32[]{:S(2)}) async-start(bf16[64,2,2,1536]{3,2,1,0:T(2,128)(2,1)} %reshape.89), calls=%async_computation.1 | async-start | bytes 1572864 | tf_op jit(solution)/shard_map/all_to_all | solution.py:87
  171.6 5.5 %collective-permute-start.1 = (f32[2,768]{1,0:T(2,128)S(1)}, f32[2,768]{1,0:T(2,128)S(1)}, u32[]{:S(2)}, u32[]{:S(2)}) collective-permute-start(f32[2,768]{1,0:T(2,128)S(1)} %convert_reduce_fusion), channel_id=1, source_target_pairs={{0,1},{1,0},{2,3},{3,2},{4,5},{5,4},{6,7},{7,6},{8,9},{9,8},{10,11... | collective-permute-start | bytes 18440 | tf_op jit(solution)/shard_map/ppermute | solution.py:18
  177.2 6.4 %collective-permute-start.2 = (f32[2,768]{1,0:T(2,128)S(1)}, f32[2,768]{1,0:T(2,128)S(1)}, u32[]{:S(2)}, u32[]{:S(2)}) collective-permute-start(f32[2,768]{1,0:T(2,128)S(1)} %add.110), channel_id=1, source_target_pairs={{0,2},{1,3},{2,0},{3,1},{4,6},{5,7},{6,4},{7,5},{8,10},{9,11},{10,... | collective-permute-start | bytes 18440 | tf_op jit(solution)/shard_map/ppermute | solution.py:18
  183.6 9.5 %collective-permute-start.3 = (f32[2,768]{1,0:T(2,128)S(1)}, f32[2,768]{1,0:T(2,128)S(1)}, u32[]{:S(2)}, u32[]{:S(2)}) collective-permute-start(f32[2,768]{1,0:T(2,128)S(1)} %add.111), channel_id=1, source_target_pairs={{0,4},{1,5},{2,6},{3,7},{4,0},{5,1},{6,2},{7,3},{8,12},{9,13},{10,... | collective-permute-start | bytes 18440 | tf_op jit(solution)/shard_map/ppermute | solution.py:18
  193.0 57.5 %collective-permute-start.4 = (f32[2,768]{1,0:T(2,128)S(1)}, f32[2,768]{1,0:T(2,128)S(1)}, u32[]{:S(2)}, u32[]{:S(2)}) collective-permute-start(f32[2,768]{1,0:T(2,128)S(1)} %add.112), channel_id=1, source_target_pairs={{0,8},{1,9},{2,10},{3,11},{4,12},{5,13},{6,14},{7,15},{8,0},{9,1},... | collective-permute-start | bytes 18440 | tf_op jit(solution)/shard_map/ppermute | solution.py:18
  199.1 5.6 %collective-permute-start.7 = (s32[1]{0:T(128)}, s32[1]{0:T(128)}, u32[]{:S(2)}, u32[]{:S(2)}) collective-permute-start(s32[1]{0:T(128)} %bitcast.13), channel_id=1, source_target_pairs={{0,1},{1,0},{2,3},{3,2},{4,5},{5,4},{6,7},{7,6},{8,9},{9,8},{10,11... | collective-permute-start | bytes 20 | tf_op jit(solution)/shard_map/ppermute | solution.py:18
  205.3 6.3 %collective-permute-start.8 = (s32[1]{0:T(128)}, s32[1]{0:T(128)}, u32[]{:S(2)}, u32[]{:S(2)}) collective-permute-start(s32[1]{0:T(128)} %add.116), channel_id=1, source_target_pairs={{0,2},{1,3},{2,0},{3,1},{4,6},{5,7},{6,4},{7,5},{8,10},{9,11},{10,... | collective-permute-start | bytes 20 | tf_op jit(solution)/shard_map/ppermute | solution.py:18
  212.2 9.3 %collective-permute-start.9 = (s32[1]{0:T(128)}, s32[1]{0:T(128)}, u32[]{:S(2)}, u32[]{:S(2)}) collective-permute-start(s32[1]{0:T(128)} %add.117), channel_id=1, source_target_pairs={{0,4},{1,5},{2,6},{3,7},{4,0},{5,1},{6,2},{7,3},{8,12},{9,13},{10,... | collective-permute-start | bytes 20 | tf_op jit(solution)/shard_map/ppermute | solution.py:18
  222.2 14.1 %collective-permute-start.10 = (s32[1]{0:T(128)}, s32[1]{0:T(128)}, u32[]{:S(2)}, u32[]{:S(2)}) collective-permute-start(s32[1]{0:T(128)} %add.118), channel_id=1, source_target_pairs={{0,8},{1,9},{2,10},{3,11},{4,12},{5,13},{6,14},{7,15},{8,0},{9,1},... | collective-permute-start | bytes 20 | tf_op jit(solution)/shard_map/ppermute | solution.py:18
  236.9 5.4 %collective-permute-start.11 = (s32[1]{0:T(128)}, s32[1]{0:T(128)}, u32[]{:S(2)}, u32[]{:S(2)}) collective-permute-start(s32[1]{0:T(128)} %add.119), channel_id=1, source_target_pairs={{0,16},{1,17},{2,18},{3,19},{4,20},{5,21},{6,22},{7,23},{8,24},{9,... | collective-permute-start | bytes 20 | tf_op jit(solution)/shard_map/ppermute | solution.py:18
  243.0 6.9 %collective-permute-start.12 = (s32[1]{0:T(128)}, s32[1]{0:T(128)}, u32[]{:S(2)}, u32[]{:S(2)}) collective-permute-start(s32[1]{0:T(128)} %add.120), channel_id=1, source_target_pairs={{0,32},{1,33},{2,34},{3,35},{4,36},{5,37},{6,38},{7,39},{8,40},{9,... | collective-permute-start | bytes 20 | tf_op jit(solution)/shard_map/ppermute | solution.py:18
  250.5 5.5 %collective-permute-start.5 = (f32[2,768]{1,0:T(2,128)S(1)}, f32[2,768]{1,0:T(2,128)S(1)}, u32[]{:S(2)}, u32[]{:S(2)}) collective-permute-start(f32[2,768]{1,0:T(2,128)S(1)} %add.113), channel_id=1, source_target_pairs={{0,16},{1,17},{2,18},{3,19},{4,20},{5,21},{6,22},{7,23},{8,24},{9,... | collective-permute-start | bytes 18440 | tf_op jit(solution)/shard_map/ppermute | solution.py:18
  256.1 7.0 %collective-permute-start.6 = (f32[2,768]{1,0:T(2,128)S(1)}, f32[2,768]{1,0:T(2,128)S(1)}, u32[]{:S(2)}, u32[]{:S(2)}) collective-permute-start(f32[2,768]{1,0:T(2,128)S(1)} %add.114), channel_id=1, source_target_pairs={{0,32},{1,33},{2,34},{3,35},{4,36},{5,37},{6,38},{7,39},{8,40},{9,... | collective-permute-start | bytes 18440 | tf_op jit(solution)/shard_map/ppermute | solution.py:18
  264.8 1.9 copy-start.2
  264.9 1.9 copy-start.3
  264.9 1.9 copy-start.4
  264.9 1.9 copy-start.5
where the time goes:
time: 270 us; the launch traced here: 268 us
  waiting for transfers between devices  143 us (53%)
  starting transfers between devices  85.7 us (32%)
  local copies, waits for them, and re-layouts  18.2 us (7%)
  other arithmetic  8.16 us (3%)
  matrix products  7.86 us (3%)
  between operations  4.75 us (2%)
    ppermute x12, starting transfers between devices, from_partner(): return lax.ppermute(value, axis, pairs)  47 us
    all_to_all x1, waiting for transfers between devices, on_device(): lax.all_to_all(solved_here, 'leaf', split_axis=0, concat_axis=0, tiled=True)  42 us
    all_to_all x1, waiting for transfers between devices, on_device(): lax.all_to_all(send, 'leaf', split_axis=0, concat_axis=0, tiled=True)  39 us
    ppermute x12, waiting for transfers between devices, from_partner(): return lax.ppermute(value, axis, pairs)  37.8 us
    ppermute x7, waiting for transfers between devices, from_behind(): lax.ppermute(value, axis, [(source, source + steps) for source in range(i...  24.6 us
    all_to_all x1, starting transfers between devices, on_device(): lax.all_to_all(send, 'leaf', split_axis=0, concat_axis=0, tiled=True)  18.4 us
    ppermute x7, starting transfers between devices, from_behind(): lax.ppermute(value, axis, [(source, source + steps) for source in range(i...  13.4 us
    scatter x1, local copies, waits for them, and re-layouts, on_device(): jnp.zeros((nleaf * capacity, shots, width2), jnp.bfloat16).at[slot].set(rhs)  8.07 us
  transfers between devices with their start and end apart: 21, of which 20 were waited for; matrix products, arithmetic and copies ran while one was open for 2% of the time, Pallas kernels for 0%

commit v1 on v0

v1 whole, which is shorter than its diff:
```python
import functools
import math

import jax
import jax.numpy as jnp
from jax import lax
from jax.experimental import pallas as pl
from jax.experimental.pallas import tpu as pltpu
from jax.sharding import PartitionSpec as P

NY = 4
ROWS = 128
MESH = pl.DeviceIdType.MESH
F32 = jnp.float32
BF16 = jnp.bfloat16


def dot(a, b):
    return jnp.dot(a, b, preferred_element_type=F32)


def kernel(
    sizes,
    src_hbm, ft_ref, trow_ref, tcol_ref, code_ref, fac_hbm, sep_hbm,
    out_ref,
    src, fac, sep, send1, sendf, recv1, recvf, face_in, acc, back1, back2, ret1, ret2, vsend, vrecv,
    load_sem, face_ss, face_rs, a2a_ss, a2a_rs, tree_ss, tree_rs,
):
    npanel, nleaf, levels, leaves = sizes
    nz = nleaf // NY
    me_p = lax.axis_index("panel")
    me = lax.axis_index("leaf")
    my_y, my_z = me // nz, me % nz

    def peer(k, sign):
        y = (my_y + sign * (k // nz) + NY) % NY
        z = (my_z + sign * (k % nz) + nz) % nz
        return {"panel": me_p, "leaf": y * nz + z}

    def panel_peer(j):
        return {"panel": (me_p + j) % npanel, "leaf": me}

    loads = [
        pltpu.make_async_copy(src_hbm, src, load_sem.at[0]),
        pltpu.make_async_copy(fac_hbm, fac, load_sem.at[1]),
        pltpu.make_async_copy(sep_hbm, sep, load_sem.at[2]),
    ]
    for load in loads:
        load.start()

    barrier = pltpu.get_barrier_semaphore()

    @pl.loop(1, nleaf)
    def _(k):
        pl.semaphore_signal(barrier, inc=1, device_id=peer(k, 1), device_id_type=MESH)

    for j in range(1, npanel):
        pl.semaphore_signal(barrier, inc=1, device_id=panel_peer(j), device_id_type=MESH)

    loads[0].wait()
    place = lax.broadcasted_iota(jnp.int32, (nleaf * 8, ROWS), 0)
    pick_re = (place == trow_ref[...]).astype(F32).astype(BF16)
    pick_im = (place == trow_ref[...] + 4).astype(F32).astype(BF16)
    packed = dot(pick_re, src[0, :, 0:640]) + dot(pick_im, src[1, :, 0:640])
    send1[...] = packed.reshape(nleaf, 8, 640).astype(BF16)
    recv1[0] = send1[0]

    pl.semaphore_wait(barrier, nleaf - 1 + npanel - 1)

    def face_copy(j):
        return pltpu.make_async_remote_copy(
            src_ref=ft_ref, dst_ref=face_in.at[j], send_sem=face_ss.at[j], recv_sem=face_rs.at[j],
            device_id=panel_peer(j), device_id_type=MESH,
        )

    for j in range(1, npanel):
        face_copy(j).start()

    def exchange(source, target, index, sign, first=1, last=None):
        @pl.loop(first, nleaf if last is None else last)
        def _(k):
            pltpu.make_async_remote_copy(
                src_ref=source.at[k], dst_ref=target.at[k], send_sem=a2a_ss.at[index],
                recv_sem=a2a_rs.at[index], device_id=peer(k, sign), device_id_type=MESH,
            ).start()

    def sent(buffer, index):
        part = buffer.at[pl.ds(1, nleaf - 1)]
        pltpu.make_async_copy(part, part, a2a_ss.at[index]).wait()

    def landed(buffer, index):
        part = buffer.at[pl.ds(1, nleaf - 1)]
        pltpu.make_async_copy(part, part, a2a_rs.at[index]).wait()

    exchange(send1, recv1, 0, 1)

    for j in range(1, npanel):
        face_copy(j).wait_recv()
    lane = lax.broadcasted_iota(jnp.int32, (ROWS, 128), 1)
    low = lane < 64

    def advance(q, arriving):
        slot = (me_p - q + npanel) % npanel
        tau = face_in[slot, 0]
        swapped = pltpu.roll(tau, 64, 1)
        tau_re = jnp.where(low, tau, swapped)
        tau_im = jnp.where(low, -swapped, tau)
        value = arriving + face_in[slot, 1]
        leaving = tau_re * value + tau_im * pltpu.roll(value, 64, 1)
        return jnp.where(q < me_p, leaving, arriving)

    arriving = jnp.zeros((ROWS, 128), F32)
    for q in range(npanel - 1):
        arriving = advance(q, arriving)
    zero = jnp.zeros((ROWS, 128), F32)
    tail_re = src[0, :, 640:768].astype(F32) + jnp.where(low, zero, pltpu.roll(arriving, 64, 1))
    tail_im = src[1, :, 640:768].astype(F32) + jnp.where(low, zero, arriving)
    packed = dot(pick_re, tail_re.astype(BF16)) + dot(pick_im, tail_im.astype(BF16))
    sendf[...] = packed.reshape(nleaf, 8, 128).astype(BF16)
    recvf[0] = sendf[0]
    exchange(sendf, recvf, 1, 1)

    loads[1].wait()
    loads[2].wait()
    landed(recv1, 0)
    rows = recv1[...].astype(F32).reshape(nleaf * 8, 640).astype(BF16)
    acc[0] = dot(rows, fac[0, 0:640, :])
    acc[1] = dot(rows, fac[1, 0:640, :])
    landed(recvf, 1)
    rows = recvf[...].astype(F32).reshape(nleaf * 8, 128).astype(BF16)
    turn = lax.broadcasted_iota(jnp.int32, (1, 8, 128), 1) < 4

    def combine(real, imag):
        width = real.shape[-1]
        real = real.reshape(-1, 8, width)
        imag = pltpu.roll(imag.reshape(-1, 8, width), 4, 1)
        sign = jnp.where(lax.broadcasted_iota(jnp.int32, imag.shape, 1) < 4, -1.0, 1.0)
        return real + sign * imag

    for half, back in ((0, back1), (1, back2)):
        cols = slice(half * 384, half * 384 + 384)
        real = acc[0, :, cols] + dot(rows, fac[0, 640:768, cols])
        imag = acc[1, :, cols] + dot(rows, fac[1, 640:768, cols])
        back[...] = combine(real, imag).astype(BF16)
        if half == 0:
            ret1[0] = back1[0]
            exchange(back1, ret1, 2, -1)
    ret2[0] = back2[0]
    cuts = [1 + (nleaf - 1) * i // 3 for i in range(4)]
    exchange(back2, ret2, 3, -1, cuts[0], cuts[1])

    landed(ret1, 2)
    total = jnp.sum(ret1[...].astype(F32), axis=0)
    eight = lax.broadcasted_iota(jnp.int32, (8, 384), 0)
    total = total + jnp.where(eight % 4 < 2, pltpu.roll(total, 6, 0), pltpu.roll(total, 2, 0))
    trace, code = total, code_ref[...]
    sums = []
    for step in range(levels // 2):
        vsend[step, :, 0:384] = trace
        vsend[step, :, 384:512] = code
        copies = []
        for j in range(1, 4):
            digit = me // 4**step % 4
            moved = (digit + 1 - 2 * (digit % 2), digit + 2 - 4 * (digit // 2), 3 - digit)[j - 1]
            other = me + (moved - digit) * 4**step
            copies.append(pltpu.make_async_remote_copy(
                src_ref=vsend.at[step], dst_ref=vrecv.at[step, j], send_sem=tree_ss.at[step, j],
                recv_sem=tree_rs.at[step, j], device_id={"panel": me_p, "leaf": other},
                device_id_type=MESH,
            ))
        for copy in copies:
            copy.start()
        if step < 2:
            exchange(back2, ret2, 3, -1, cuts[step + 1], cuts[step + 2])
        for copy in copies:
            copy.wait()
        pair_t = trace + vrecv[step, 1, :, 0:384]
        pair_c = code + vrecv[step, 1, :, 384:512]
        trace = pair_t + (vrecv[step, 2, :, 0:384] + vrecv[step, 3, :, 0:384])
        code = pair_c + (vrecv[step, 2, :, 384:512] + vrecv[step, 3, :, 384:512])
        sums += [(pair_t, pair_c), (trace, code)]

    sign8 = jnp.where(eight < 4, -1.0, 1.0)
    value = jnp.zeros((8, 384), F32)
    for level in reversed(range(levels)):
        level_sum, level_code = sums[level]
        odd = level_code - 2.0 * jnp.floor(level_code * 0.5)
        odd = jnp.concatenate([odd, odd, odd], axis=1) > 0.5
        scale = 1.0 / math.sqrt(leaves * 2 ** (level + 1))
        operand = (level_sum * scale - value).astype(BF16)
        real = jnp.where(odd, dot(operand, sep[1, 0]), dot(operand, sep[0, 0]))
        imag = jnp.where(odd, dot(operand, sep[1, 1]), dot(operand, sep[0, 1]))
        value = real + sign8 * pltpu.roll(imag, 4, 0)

    spot = lax.broadcasted_iota(jnp.int32, (ROWS, nleaf * 8), 1)
    even = lax.broadcasted_iota(jnp.int32, (ROWS, 384), 0) % 2 == 0
    take = [(spot == tcol_ref[...] + 4 * part).astype(F32).astype(BF16) for part in range(2)]
    rows = ret1[...].astype(F32).reshape(nleaf * 8, 384).astype(BF16)
    for part in range(2):
        shift = jnp.where(even, value[4 * part : 4 * part + 1], value[4 * part + 1 : 4 * part + 2])
        out_ref[:, 768 * part : 768 * part + 384] = (dot(take[part], rows) - shift).astype(BF16)
    landed(ret2, 3)
    rows = ret2[...].astype(F32).reshape(nleaf * 8, 384).astype(BF16)
    for part in range(2):
        out_ref[:, 768 * part + 384 : 768 * part + 768] = dot(take[part], rows).astype(BF16)

    for buffer, index in ((send1, 0), (sendf, 1), (back1, 2), (back2, 3)):
        sent(buffer, index)
    for j in range(1, npanel):
        face_copy(j).wait_send()


def on_device(sources, transmission, media, sep_code, leaf_factors, sep_factors):
    leaves, shots, width2 = sources.shape[1:]
    npanel, nleaf = lax.axis_size("panel"), lax.axis_size("leaf")
    levels = nleaf.bit_length() - 1
    nz = nleaf // NY
    me = lax.axis_index("leaf")
    used = leaves * shots
    source = sources[0].reshape(used, 2, width2 // 2)
    source = jnp.pad(source, ((0, ROWS - used), (0, 0), (0, 0))).transpose(1, 0, 2)
    face = jnp.concatenate([source[0, :, 704:], source[1, :, 704:]], axis=1).astype(F32)
    tau = jnp.pad(jnp.repeat(transmission[0], shots, axis=0), ((0, ROWS - used), (0, 0)))
    ft = jnp.stack([tau, face])
    kinds = media[0, :, 0]
    order = jnp.arange(leaves)
    twin = (kinds[:, None] == kinds[None, :]) & (order[None, :] < order[:, None])
    rank = jnp.sum(twin.astype(jnp.int32), axis=1)
    away = (kinds // nz - me // nz) % NY * nz + (kinds % nz - me % nz) % nz
    slot = (away * 8 + rank * 2)[:, None] + jnp.arange(shots)[None, :]
    slot = jnp.pad(slot.reshape(used), (0, ROWS - used), constant_values=-64)
    code = jnp.broadcast_to(sep_code.astype(F32), (8, 128))
    half = width2 // 2
    sem = pltpu.SemaphoreType.DMA
    vmem = pl.BlockSpec(memory_space=pltpu.VMEM)
    hbm = pl.BlockSpec(memory_space=pl.ANY)
    out = pl.pallas_call(
        functools.partial(kernel, (npanel, nleaf, levels, leaves)),
        out_shape=jax.ShapeDtypeStruct((ROWS, width2), BF16),
        in_specs=[hbm, vmem, vmem, vmem, vmem, hbm, hbm],
        out_specs=vmem,
        scratch_shapes=[
            pltpu.VMEM((2, ROWS, half), BF16),
            pltpu.VMEM((2, half, half), BF16),
            pltpu.VMEM(sep_factors.shape, BF16),
            pltpu.VMEM((nleaf, 8, 640), BF16),
            pltpu.VMEM((nleaf, 8, 128), BF16),
            pltpu.VMEM((nleaf, 8, 640), BF16),
            pltpu.VMEM((nleaf, 8, 128), BF16),
            pltpu.VMEM((npanel, 2, ROWS, 128), F32),
            pltpu.VMEM((2, nleaf * 8, half), F32),
            pltpu.VMEM((nleaf, 8, 384), BF16),
            pltpu.VMEM((nleaf, 8, 384), BF16),
            pltpu.VMEM((nleaf, 8, 384), BF16),
            pltpu.VMEM((nleaf, 8, 384), BF16),
            pltpu.VMEM((levels // 2, 8, 512), F32),
            pltpu.VMEM((levels // 2, 4, 8, 512), F32),
            sem((3,)), sem((npanel,)), sem((npanel,)), sem((4,)), sem((4,)),
            sem((levels // 2, 4)), sem((levels // 2, 4)),
        ],
        compiler_params=pltpu.CompilerParams(
            collective_id=0, has_side_effects=True, vmem_limit_bytes=48 * 1024 * 1024
        ),
    )(source, ft, slot[None, :], slot[:, None], code, leaf_factors[0], sep_factors)
    return out[:used].reshape(1, leaves, shots, width2)


def solution(mesh):
    return jax.shard_map(
        on_device,
        mesh=mesh,
        in_specs=(
            P("panel", "leaf", None, None),
            P("panel", "leaf", None),
            P("panel", "leaf", None),
            P("panel", "leaf"),
            P("leaf", None, None, None),
            P(),
        ),
        out_specs=P("panel", "leaf", None, None),
        check_vma=False,
    )
```

time: 270 us -> 113 us (0.42)
  the two profiles are of different devices: /device:TPU:36 before, /device:TPU:4 now
where the time goes in v1:
time: 113 us
  Pallas kernels  106 us (94%)
  local copies, waits for them, and re-layouts  4.48 us (4%)
  other arithmetic  1.76 us (2%)
    pallas_call x1, Pallas kernels, on_device(): pl.pallas_call(functools.partial(kernel, (npanel, nleaf, levels, leaves))...  106 us

profile of v1, /device:TPU:4, one launch (start us, length us, event | category | flops | bytes accessed | tf_op | source)
XLA Modules:
  0.0 112.9 jit_solution(9633510415581776072)
XLA Ops:
  0.0 0.0 copy-start
  0.8 0.9 convert_reduce_fusion
  1.7 0.7 multiply_add_fusion
  2.4 0.1 iota_add_fusion
  2.5 0.1 add.82
  2.6 0.7 copy.14
  3.4 0.1 copy.11.tcol_ref
  3.5 1.2 %reshape_squeeze.3 = bf16[104,2,768]{2,1,0:T(2,128)(2,1)S(1)} reshape(bf16[1,52,2,1536]{3,2,1,0:T(2,128)(2,1)} %param.6) | data formatting | bytes 638976 | tf_op jit(solution)/shard_map/reshape;squeeze | solution.py:220
  4.8 0.1 fusion.6
  4.9 0.1 maximum_convert_fusion
  5.0 0.0 copy-done
  5.0 0.0 copy-start.1
  5.0 1.3 %copy-done.1 = bf16[2,2,384,384]{3,2,1,0:T(8,128)(2,1)S(1)} copy-done((bf16[2,2,384,384]{3,2,1,0:T(8,128)(2,1)S(1)}, bf16[2,2,384,384]{3,2,1,0:T(8,128)(2,1)}, u32[]{:S(2)}) %copy-start.1) | copy-done | bytes 1179672
  6.3 105.7 %shard_map.64 = bf16[128,1536]{1,0:T(8,128)(2,1)S(1)} custom-call(bf16[2,128,768]{2,1,0:T(8,128)(2,1)S(1)} %pad_bitcast_fusion.src_hbm, f32[2,128,128]{2,1,0:T(8,128)S(1)} %pad_maximum_fusion.ft_ref, s32[1,128]{1,0:T(1,128)S(1)} %get-tuple-element.8.trow_ref, s32[128,1]{1,0:T(8,128)S(1)} %copy.11.tcol_ref, f32[8,128]{1,0:T(8,128)S(1)} %broadcast_in_dim.24.code_ref, ...), custom_call_target="tpu_custom_call" | custom-call | tf_op jit(solution)/shard_map/pallas_call | solution.py:237
  112.0 0.8 reshape.117
  (8 shorter events, 0.1 us)
Async XLA Ops:
  0.0 5.0 %copy-start = (bf16[1,2,768,768]{3,2,1,0:T(8,128)(2,1)S(1)}, bf16[1,2,768,768]{3,2,1,0:T(8,128)(2,1)}, u32[]{:S(2)}) copy-start(bf16[1,2,768,768]{3,2,1,0:T(8,128)(2,1)} %param.10) | copy-start | bytes 7077892
  5.0 1.3 %copy-start.1 = (bf16[2,2,384,384]{3,2,1,0:T(8,128)(2,1)S(1)}, bf16[2,2,384,384]{3,2,1,0:T(8,128)(2,1)}, u32[]{:S(2)}) copy-start(bf16[2,2,384,384]{3,2,1,0:T(8,128)(2,1)} %sep_hbm.1) | copy-start | bytes 3538948

commit v2 on v1

v2 whole, which is shorter than its diff:
```python
import functools
import math

import jax
import jax.numpy as jnp
from jax import lax
from jax.experimental import pallas as pl
from jax.experimental.pallas import tpu as pltpu
from jax.sharding import PartitionSpec as P

NY = 4
ROWS = 112
MESH = pl.DeviceIdType.MESH
F32 = jnp.float32
BF16 = jnp.bfloat16
I32 = jnp.int32


def dot(a, b):
    return jnp.dot(a, b, preferred_element_type=F32)


def iota(shape, axis):
    return lax.broadcasted_iota(I32, shape, axis)


def kernel(
    sizes,
    src_hbm, tau_hbm, media_hbm, code_hbm, fac_hbm, sep_hbm,
    out_ref,
    tau_ref, media_ref, code_ref, raw, src, fac, sep, send, recv, tau_out, face_out, tau_in, face_in, back1, back2, ret1, ret2,
    csend, crecv, vsend, vrecv, chosen, top,
    load_sem, tau_ss, tau_rs, face_ss, face_rs, a2a_ss, a2a_rs, code_ss, code_rs, tree_ss, tree_rs,
):
    npanel, nleaf, levels, leaves = sizes
    nz = nleaf // NY
    used = 2 * leaves
    rounds = levels // 2
    me_p = lax.axis_index("panel")
    me = lax.axis_index("leaf")
    my_y, my_z = me // nz, me % nz

    def peer(k, sign):
        y = (my_y + sign * (k // nz) + NY) % NY
        z = (my_z + sign * (k % nz) + nz) % nz
        return {"panel": me_p, "leaf": y * nz + z}

    def panel_peer(j):
        return {"panel": (me_p + j) % npanel, "leaf": me}

    barrier = pltpu.get_barrier_semaphore()

    @pl.loop(1, nleaf)
    def _(k):
        pl.semaphore_signal(barrier, inc=1, device_id=peer(k, 1), device_id_type=MESH)

    for j in range(1, npanel):
        pl.semaphore_signal(barrier, inc=1, device_id=panel_peer(j), device_id_type=MESH)

    loads = [
        pltpu.make_async_copy(src_hbm.at[0], raw, load_sem.at[0]),
        pltpu.make_async_copy(fac_hbm.at[0], fac, load_sem.at[1]),
        pltpu.make_async_copy(sep_hbm, sep, load_sem.at[2]),
        pltpu.make_async_copy(media_hbm, media_ref, load_sem.at[3]),
        pltpu.make_async_copy(tau_hbm, tau_ref, load_sem.at[4]),
        pltpu.make_async_copy(code_hbm, code_ref, load_sem.at[5]),
    ]
    for load in loads:
        load.start()

    for load in loads[3:]:
        load.wait()
    lane = iota((ROWS, leaves), 1)
    leaf = iota((ROWS, leaves), 0) // 2
    kinds = jnp.broadcast_to(media_ref[...], (ROWS, leaves)).astype(F32)
    kind = jnp.sum(jnp.where(lane == leaf, kinds, 0.0), axis=1, keepdims=True)
    rank = jnp.sum(jnp.where((kinds == kind) & (lane < leaf), 1.0, 0.0), axis=1, keepdims=True)
    kind, rank = kind.astype(I32), rank.astype(I32)
    row = iota((ROWS, 1), 0)
    away_y = (kind // nz - my_y + NY) % NY
    away_z = (kind % nz - my_z + nz) % nz
    spot = (away_y * nz + away_z) * 8 + rank * 2 + row % 2
    spot = jnp.where(row < used, spot, -64)
    diagonal = iota((ROWS, ROWS), 0) == iota((ROWS, ROWS), 1)
    spot_row = jnp.sum(jnp.where(diagonal, spot.astype(F32), 0.0), axis=0, keepdims=True).astype(I32)
    place = iota((nleaf * 8, ROWS), 0)
    pick = [(place == spot_row + 4 * part).astype(F32).astype(BF16) for part in range(2)]

    tau_out[0:leaves, :] = tau_ref[...].reshape(leaves, 128)
    tau_out[leaves:56, :] = jnp.zeros((56 - leaves, 128), F32)
    loads[0].wait()
    rows = raw[...].astype(F32).reshape(used, 1536)
    src[...] = jnp.concatenate([rows, jnp.zeros((ROWS - used, 1536), F32)], axis=0).astype(BF16)
    low = iota((ROWS, 128), 1) < 64
    tile_re, tile_im = src[:, 640:768].astype(F32), src[:, 1408:1536].astype(F32)
    face_out[...] = jnp.where(low, pltpu.roll(tile_re, 64, 1), tile_im).astype(BF16)
    packed = dot(pick[0], src[:, 0:640]) + dot(pick[1], src[:, 768:1408])
    send[:, :, 0:640] = packed.reshape(nleaf, 8, 640).astype(BF16)
    csend[0] = jnp.broadcast_to(code_ref[...].astype(F32), (8, 128))

    pl.semaphore_wait(barrier, nleaf - 1 + npanel - 1)

    def face_copies(j):
        return [
            pltpu.make_async_remote_copy(
                src_ref=tau_out, dst_ref=tau_in.at[j], send_sem=tau_ss.at[j],
                recv_sem=tau_rs.at[j], device_id=panel_peer(j), device_id_type=MESH,
            ),
            pltpu.make_async_remote_copy(
                src_ref=face_out, dst_ref=face_in.at[j], send_sem=face_ss.at[j],
                recv_sem=face_rs.at[j], device_id=panel_peer(j), device_id_type=MESH,
            ),
        ]

    for j in range(1, npanel):
        for copy in face_copies(j):
            copy.start()

    def exchange(source, target, index, sign, first, last, cols):
        @pl.loop(max(first, 1), last)
        def _(k):
            pltpu.make_async_remote_copy(
                src_ref=source.at[k, :, cols], dst_ref=target.at[k, :, cols],
                send_sem=a2a_ss.at[index], recv_sem=a2a_rs.at[index],
                device_id=peer(k, sign), device_id_type=MESH,
            ).start()

    def wait_for(sems, buffer, index, first, last, cols):
        part = buffer.at[pl.ds(max(first, 1), last - max(first, 1)), :, cols]
        pltpu.make_async_copy(part, part, sems.at[index]).wait()

    def tree_copies(step, source, target, ss, rs):
        copies = []
        for j in range(1, 4):
            digit = me // 4**step % 4
            moved = (digit + 1 - 2 * (digit % 2), digit + 2 - 4 * (digit // 2), 3 - digit)[j - 1]
            other = me + (moved - digit) * 4**step
            copies.append(pltpu.make_async_remote_copy(
                src_ref=source.at[step], dst_ref=target.at[step, j], send_sem=ss.at[step, j],
                recv_sem=rs.at[step, j], device_id={"panel": me_p, "leaf": other},
                device_id_type=MESH,
            ))
        return copies

    def two_levels(own, got, step):
        pair = own + got[step, 1]
        return pair, pair + (got[step, 2] + got[step, 3])

    bulk, tail, whole = pl.ds(0, 640), pl.ds(640, 128), pl.ds(0, 768)
    half = pl.ds(0, 384)
    cuts = [nleaf * i // 4 for i in range(5)]
    early = 2
    codes = []
    for step in range(rounds):
        copies = tree_copies(step, csend, crecv, code_ss, code_rs)
        for copy in copies:
            copy.start()
        if step < early:
            exchange(send, recv, step, 1, cuts[step], cuts[step + 1], bulk)
        for copy in copies:
            copy.wait()
        codes += two_levels(csend[step], crecv, step)
        if step + 1 < rounds:
            csend[step + 1] = codes[-1]

    for j in range(1, npanel):
        for copy in face_copies(j):
            copy.wait_recv()
    arriving = jnp.zeros((ROWS, 128), F32)
    for q in range(npanel - 1):
        slot = (me_p - q + npanel) % npanel
        tau = jnp.broadcast_to(tau_in[slot].reshape(56, 1, 128), (56, 2, 128)).reshape(ROWS, 128)
        swapped = pltpu.roll(tau, 64, 1)
        tau_re = jnp.where(low, tau, swapped)
        tau_im = jnp.where(low, -swapped, tau)
        value = arriving + face_in[slot].astype(F32)
        leaving = tau_re * value + tau_im * pltpu.roll(value, 64, 1)
        arriving = jnp.where(q < me_p, leaving, arriving)
    zero = jnp.zeros((ROWS, 128), F32)
    tile_re = src[:, 640:768].astype(F32) + jnp.where(low, zero, pltpu.roll(arriving, 64, 1))
    tile_im = src[:, 1408:1536].astype(F32) + jnp.where(low, zero, arriving)
    packed = dot(pick[0], tile_re.astype(BF16)) + dot(pick[1], tile_im.astype(BF16))
    send[:, :, 640:768] = packed.reshape(nleaf, 8, 128).astype(BF16)
    recv[0] = send[0]
    for g in range(early):
        exchange(send, recv, 4 + g, 1, cuts[g], cuts[g + 1], tail)
    for g in range(early, 4):
        exchange(send, recv, g, 1, cuts[g], cuts[g + 1], whole)

    loads[1].wait()
    loads[2].wait()
    for level in range(levels):
        count = codes[level][0:1, 0:1]
        odd = (count - 2.0 * jnp.floor(count * 0.5)).astype(BF16)
        odd = jnp.broadcast_to(odd, (384, 384))
        for part in range(2):
            chosen[level, :, 384 * part : 384 * part + 384] = (
                sep[0, part] * (1 - odd) + sep[1, part] * odd
            )

    def combine(real, imag):
        real = real.reshape(-1, 8, 384)
        imag = pltpu.roll(imag.reshape(-1, 8, 384), 4, 1)
        return real + jnp.where(iota(imag.shape, 1) < 4, -1.0, 1.0) * imag

    for g in range(4):
        first, last = cuts[g], cuts[g + 1]
        wait_for(a2a_rs, recv, g, first, last, bulk if g < early else whole)
        if g < early:
            wait_for(a2a_rs, recv, 4 + g, first, last, tail)
        rows = recv[first:last].astype(F32).reshape((last - first) * 8, 768).astype(BF16)
        for part, back in ((0, back1), (1, back2)):
            cols = slice(part * 384, part * 384 + 384)
            result = combine(dot(rows, fac[0, :, cols]), dot(rows, fac[1, :, cols]))
            back[first:last] = result.astype(BF16)
            if part == 0:
                exchange(back1, ret1, 6 + g, -1, first, last, half)
    ret1[0] = back1[0]
    ret2[0] = back2[0]
    turns = [1, 12, 24, 46, nleaf]
    exchange(back2, ret2, 10, -1, turns[0], turns[1], half)

    for g in range(4):
        wait_for(a2a_rs, ret1, 6 + g, cuts[g], cuts[g + 1], half)
    total = jnp.sum(ret1[...].astype(F32), axis=0)
    eight = iota((8, 384), 0)
    total = total + jnp.where(eight % 4 < 2, pltpu.roll(total, 6, 0), pltpu.roll(total, 2, 0))
    sums = []
    spots = iota((ROWS, nleaf * 8), 1)
    take = [(spots == spot + 4 * part).astype(F32).astype(BF16) for part in range(2)]
    for step in range(rounds):
        vsend[step] = total
        copies = tree_copies(step, vsend, vrecv, tree_ss, tree_rs)
        for copy in copies:
            copy.start()
        exchange(back2, ret2, 10, -1, turns[step + 1], turns[step + 2], half)
        if step == 0:
            rows = ret1[...].astype(F32).reshape(nleaf * 8, 384).astype(BF16)
            for part in range(2):
                top[part] = dot(take[part], rows)
        for copy in copies:
            copy.wait()
        sums += two_levels(total, vrecv, step)
        total = sums[-1]

    sign8 = jnp.where(eight < 4, -1.0, 1.0)
    value = jnp.zeros((8, 384), F32)
    for level in reversed(range(levels)):
        scale = 1.0 / math.sqrt(leaves * 2 ** (level + 1))
        operand = (sums[level] * scale - value).astype(BF16)
        both = dot(operand, chosen[level])
        value = both[:, 0:384] + sign8 * pltpu.roll(both[:, 384:768], 4, 0)

    even = iota((ROWS, 384), 0) % 2 == 0
    for part in range(2):
        shift = jnp.where(even, value[4 * part : 4 * part + 1], value[4 * part + 1 : 4 * part + 2])
        out_ref[:, 768 * part : 768 * part + 384] = (top[part] - shift).astype(BF16)
    wait_for(a2a_rs, ret2, 10, 0, nleaf, half)
    rows = ret2[...].astype(F32).reshape(nleaf * 8, 384).astype(BF16)
    for part in range(2):
        out_ref[:, 768 * part + 384 : 768 * part + 768] = dot(take[part], rows).astype(BF16)

    for g in range(4):
        wait_for(a2a_ss, send, g, cuts[g], cuts[g + 1], bulk if g < early else whole)
        if g < early:
            wait_for(a2a_ss, send, 4 + g, cuts[g], cuts[g + 1], tail)
        wait_for(a2a_ss, back1, 6 + g, cuts[g], cuts[g + 1], half)
    wait_for(a2a_ss, back2, 10, 0, nleaf, half)
    for j in range(1, npanel):
        for copy in face_copies(j):
            copy.wait_send()


def on_device(sources, transmission, media, sep_code, leaf_factors, sep_factors):
    leaves, shots, width2 = sources.shape[1:]
    npanel, nleaf = lax.axis_size("panel"), lax.axis_size("leaf")
    levels = nleaf.bit_length() - 1
    rounds = levels // 2
    half = width2 // 2
    sem = pltpu.SemaphoreType.DMA
    vmem = pl.BlockSpec(memory_space=pltpu.VMEM)
    hbm = pl.BlockSpec(memory_space=pl.ANY)
    out = pl.pallas_call(
        functools.partial(kernel, (npanel, nleaf, levels, leaves)),
        out_shape=jax.ShapeDtypeStruct((ROWS, width2), BF16),
        in_specs=[hbm] * 6,
        out_specs=vmem,
        scratch_shapes=[
            pltpu.VMEM((leaves, 1, 128), F32),
            pltpu.VMEM((1, leaves), I32),
            pltpu.VMEM((1, 1), I32),
            pltpu.VMEM((leaves, shots, width2), BF16),
            pltpu.VMEM((ROWS, width2), BF16),
            pltpu.VMEM((2, half, half), BF16),
            pltpu.VMEM(sep_factors.shape, BF16),
            pltpu.VMEM((nleaf, 8, half), BF16),
            pltpu.VMEM((nleaf, 8, half), BF16),
            pltpu.VMEM((ROWS // 2, 128), F32),
            pltpu.VMEM((ROWS, 128), BF16),
            pltpu.VMEM((npanel, ROWS // 2, 128), F32),
            pltpu.VMEM((npanel, ROWS, 128), BF16),
            pltpu.VMEM((nleaf, 8, 384), BF16),
            pltpu.VMEM((nleaf, 8, 384), BF16),
            pltpu.VMEM((nleaf, 8, 384), BF16),
            pltpu.VMEM((nleaf, 8, 384), BF16),
            pltpu.VMEM((rounds, 8, 128), F32),
            pltpu.VMEM((rounds, 4, 8, 128), F32),
            pltpu.VMEM((rounds, 8, 384), F32),
            pltpu.VMEM((rounds, 4, 8, 384), F32),
            pltpu.VMEM((levels, 384, 768), BF16),
            pltpu.VMEM((2, ROWS, 384), F32),
            sem((6,)), sem((npanel,)), sem((npanel,)), sem((npanel,)), sem((npanel,)),
            sem((11,)), sem((11,)), sem((rounds, 4)), sem((rounds, 4)), sem((rounds, 4)),
            sem((rounds, 4)),
        ],
        compiler_params=pltpu.CompilerParams(
            collective_id=0, has_side_effects=True, vmem_limit_bytes=67043328
        ),
    )(
        sources, transmission.transpose(1, 0, 2), media.reshape(1, leaves), sep_code,
        leaf_factors, sep_factors,
    )
    return out[: leaves * shots].reshape(1, leaves, shots, width2)


def solution(mesh):
    return jax.shard_map(
        on_device,
        mesh=mesh,
        in_specs=(
            P("panel", "leaf", None, None),
            P("panel", "leaf", None),
            P("panel", "leaf", None),
            P("panel", "leaf"),
            P("leaf", None, None, None),
            P(),
        ),
        out_specs=P("panel", "leaf", None, None),
        check_vma=False,
    )
```

time: 113 us -> 105 us (0.929)
  the two profiles are of different devices: /device:TPU:4 before, /device:TPU:16 now
where the time goes in v2:
time: 105 us
  Pallas kernels  103 us (98%)
  local copies, waits for them, and re-layouts  1.83 us (2%)
    pallas_call x1, Pallas kernels, on_device(): pl.pallas_call(functools.partial(kernel, (npanel, nleaf, levels, leaves))...  103 us

profile of v2, /device:TPU:16, one launch (start us, length us, event | category | flops | bytes accessed | tf_op | source)
XLA Modules:
  0.0 105.3 jit_solution(18180110546959975308)
XLA Ops:
  0.7 102.8 %shard_map.64 = bf16[112,1536]{1,0:T(8,128)(2,1)} custom-call(bf16[1,52,2,1536]{3,2,1,0:T(2,128)(2,1)} %src_hbm.1, f32[52,1,128]{2,1,0:T(1,128)} %bitcast.2, s32[1,52]{1,0:T(1,128)} %bitcast.3, s32[1,1]{1,0:T(1,128)S(6)} %copy.7.code_hbm, bf16[1,2,768,768]{3,2,1,0:T(8,128)(2,1)} %fac_hbm.1, bf16[2,2,384,384]{3,2,1,0:T(8,128)(2,1)} %sep_hbm.1), custom_call_target="tpu_custom_call" | custom-call | tf_op jit(solution)/shard_map/pallas_call | solution.py:283
  103.4 1.0 slice.3
  104.4 0.8 reshape.7

commit v3 on v2

--- a/solution.py
+++ b/solution.py
@@ -29,8 +29,9 @@
     src_hbm, tau_hbm, media_hbm, code_hbm, fac_hbm, sep_hbm,
     out_ref,
     tau_ref, media_ref, code_ref, raw, src, fac, sep, send, recv, tau_out, face_out, tau_in, face_in, back1, back2, ret1, ret2,
-    csend, crecv, vsend, vrecv, chosen, top,
-    load_sem, tau_ss, tau_rs, face_ss, face_rs, a2a_ss, a2a_rs, code_ss, code_rs, tree_ss, tree_rs,
+    csend, crecv, vsend, vrecv, ysend, esend, erecv, chosen, top,
+    far_sem, load_sem, tau_ss, tau_rs, face_ss, face_rs, a2a_ss, a2a_rs, code_ss, code_rs, tree_ss, tree_rs,
+    node_ss, node_rs,
 ):
     npanel, nleaf, levels, leaves = sizes
     nz = nleaf // NY
@@ -41,16 +42,21 @@
     my_y, my_z = me // nz, me % nz
 
     def peer(k, sign):
-        y = (my_y + sign * (k // nz) + NY) % NY
-        z = (my_z + sign * (k % nz) + nz) % nz
+        order = k // NY
+        steps = (order % 2) * ((order + 1) // 2) - (1 - order % 2) * (order // 2)
+        y = (my_y + sign * (k % NY) + NY) % NY
+        z = (my_z + sign * steps + nz) % nz
         return {"panel": me_p, "leaf": y * nz + z}
+
+    reach = nz // 4
+    near = (2 * reach + 1) * NY
 
     def panel_peer(j):
         return {"panel": (me_p + j) % npanel, "leaf": me}
 
     barrier = pltpu.get_barrier_semaphore()
 
-    @pl.loop(1, nleaf)
+    @pl.loop(1, near)
     def _(k):
         pl.semaphore_signal(barrier, inc=1, device_id=peer(k, 1), device_id_type=MESH)
 
@@ -79,7 +85,9 @@
     row = iota((ROWS, 1), 0)
     away_y = (kind // nz - my_y + NY) % NY
     away_z = (kind % nz - my_z + nz) % nz
-    spot = (away_y * nz + away_z) * 8 + rank * 2 + row % 2
+    order = jnp.where(away_z <= nz // 2, 2 * away_z - 1, 2 * (nz - away_z))
+    order = jnp.maximum(order, 0)
+    spot = (order * NY + away_y) * 8 + rank * 2 + row % 2
     spot = jnp.where(row < used, spot, -64)
     diagonal = iota((ROWS, ROWS), 0) == iota((ROWS, ROWS), 1)
     spot_row = jnp.sum(jnp.where(diagonal, spot.astype(F32), 0.0), axis=0, keepdims=True).astype(I32)
@@ -98,7 +106,9 @@
     send[:, :, 0:640] = packed.reshape(nleaf, 8, 640).astype(BF16)
     csend[0] = jnp.broadcast_to(code_ref[...].astype(F32), (8, 128))
 
-    pl.semaphore_wait(barrier, nleaf - 1 + npanel - 1)
+    pl.semaphore_wait(barrier, near - 1 + npanel - 1)
+    for order in (2 * reach - 1, 2 * reach):
+        pl.semaphore_signal(far_sem, inc=1, device_id=peer(order * NY, 1), device_id_type=MESH)
 
     def face_copies(j):
         return [
@@ -148,20 +158,28 @@
 
     bulk, tail, whole = pl.ds(0, 640), pl.ds(640, 128), pl.ds(0, 768)
     half = pl.ds(0, 384)
-    cuts = [nleaf * i // 4 for i in range(5)]
-    early = 2
+    cuts = [0, near, (near + nleaf) // 2 + 2, nleaf]
+    groups = len(cuts) - 1
     codes = []
-    for step in range(rounds):
+
+    def code_round(step):
         copies = tree_copies(step, csend, crecv, code_ss, code_rs)
         for copy in copies:
             copy.start()
-        if step < early:
-            exchange(send, recv, step, 1, cuts[step], cuts[step + 1], bulk)
+        return copies
+
+    def code_levels(step, copies):
         for copy in copies:
             copy.wait()
-        codes += two_levels(csend[step], crecv, step)
+        codes.extend(two_levels(csend[step], crecv, step))
         if step + 1 < rounds:
             csend[step + 1] = codes[-1]
+
+    copies = code_round(0)
+    exchange(send, recv, 0, 1, 0, near, bulk)
+    pl.semaphore_wait(far_sem, 2)
+    code_levels(0, copies)
+    copies = code_round(1)
 
     for j in range(1, npanel):
         for copy in face_copies(j):
@@ -182,10 +200,14 @@
     packed = dot(pick[0], tile_re.astype(BF16)) + dot(pick[1], tile_im.astype(BF16))
     send[:, :, 640:768] = packed.reshape(nleaf, 8, 128).astype(BF16)
     recv[0] = send[0]
-    for g in range(early):
-        exchange(send, recv, 4 + g, 1, cuts[g], cuts[g + 1], tail)
-    for g in range(early, 4):
-        exchange(send, recv, g, 1, cuts[g], cuts[g + 1], whole)
+    exchange(send, recv, 4, 1, 0, near, tail)
+    exchange(send, recv, 1, 1, cuts[1], cuts[2], whole)
+    code_levels(1, copies)
+    if rounds > 2:
+        copies = code_round(2)
+    exchange(send, recv, 2, 1, cuts[2], cuts[3], whole)
+    if rounds > 2:
+        code_levels(2, copies)
 
     loads[1].wait()
     loads[2].wait()
@@ -203,10 +225,11 @@
         imag = pltpu.roll(imag.reshape(-1, 8, 384), 4, 1)
         return real + jnp.where(iota(imag.shape, 1) < 4, -1.0, 1.0) * imag
 
-    for g in range(4):
+    by_row = jnp.zeros((NY, 8, 384), F32)
+    for g in range(groups):
         first, last = cuts[g], cuts[g + 1]
-        wait_for(a2a_rs, recv, g, first, last, bulk if g < early else whole)
-        if g < early:
+        wait_for(a2a_rs, recv, g, first, last, bulk if g == 0 else whole)
+        if g == 0:
             wait_for(a2a_rs, recv, 4 + g, first, last, tail)
         rows = recv[first:last].astype(F32).reshape((last - first) * 8, 768).astype(BF16)
         for part, back in ((0, back1), (1, back2)):
@@ -215,33 +238,72 @@
             back[first:last] = result.astype(BF16)
             if part == 0:
                 exchange(back1, ret1, 6 + g, -1, first, last, half)
+                solved = back1[first:last].astype(F32).reshape(-1, NY, 8, 384)
+                by_row = by_row + jnp.sum(solved, axis=0)
     ret1[0] = back1[0]
     ret2[0] = back2[0]
-    turns = [1, 12, 24, 46, nleaf]
+    eight = iota((8, 384), 0)
+
+    def both_slots(rows):
+        other = jnp.where(eight % 4 < 2, pltpu.roll(rows, 6, 0), pltpu.roll(rows, 2, 0))
+        return rows + other
+
+    for j in range(NY):
+        ysend[j] = both_slots(by_row[j])
+    row_copies = [
+        pltpu.make_async_remote_copy(
+            src_ref=ysend.at[j], dst_ref=erecv.at[3, j], send_sem=node_ss.at[3, j],
+            recv_sem=node_rs.at[3, j], device_id=peer(j, -1), device_id_type=MESH,
+        )
+        for j in range(1, NY)
+    ]
+    for copy in row_copies:
+        copy.start()
+    for copy in row_copies:
+        copy.wait()
+
+    def node_round(step, value):
+        esend[step] = value
+        copies = tree_copies(step, esend, erecv, node_ss, node_rs)
+        for copy in copies:
+            copy.start()
+        return copies
+
+    turns = [1, 44, 64, 64]
+    copies = node_round(0, ysend[0] + erecv[3, 1] + (erecv[3, 2] + erecv[3, 3]))
     exchange(back2, ret2, 10, -1, turns[0], turns[1], half)
 
-    for g in range(4):
+    for g in range(groups):
         wait_for(a2a_rs, ret1, 6 + g, cuts[g], cuts[g + 1], half)
-    total = jnp.sum(ret1[...].astype(F32), axis=0)
-    eight = iota((8, 384), 0)
-    total = total + jnp.where(eight % 4 < 2, pltpu.roll(total, 6, 0), pltpu.roll(total, 2, 0))
-    sums = []
+    vsend[0] = both_slots(jnp.sum(ret1[...].astype(F32), axis=0))
+    trace_copies = tree_copies(0, vsend, vrecv, tree_ss, tree_rs)
+    for copy in trace_copies:
+        copy.start()
+    for copy in copies:
+        copy.wait()
+    copies = node_round(1, two_levels(esend[0], erecv, 0)[1])
+    exchange(back2, ret2, 10, -1, turns[1], turns[2], half)
     spots = iota((ROWS, nleaf * 8), 1)
     take = [(spots == spot + 4 * part).astype(F32).astype(BF16) for part in range(2)]
-    for step in range(rounds):
-        vsend[step] = total
-        copies = tree_copies(step, vsend, vrecv, tree_ss, tree_rs)
-        for copy in copies:
-            copy.start()
-        exchange(back2, ret2, 10, -1, turns[step + 1], turns[step + 2], half)
-        if step == 0:
-            rows = ret1[...].astype(F32).reshape(nleaf * 8, 384).astype(BF16)
-            for part in range(2):
-                top[part] = dot(take[part], rows)
-        for copy in copies:
-            copy.wait()
-        sums += two_levels(total, vrecv, step)
-        total = sums[-1]
+    rows = ret1[...].astype(F32).reshape(nleaf * 8, 384).astype(BF16)
+    for part in range(2):
+        top[part] = dot(take[part], rows)
+    for copy in trace_copies:
+        copy.wait()
+    sums = list(two_levels(vsend[0], vrecv, 0))
+    vsend[1] = sums[1]
+    beside = tree_copies(1, vsend, vrecv, tree_ss, tree_rs)[0]
+    beside.start()
+    exchange(back2, ret2, 10, -1, turns[2], turns[3], half)
+    for copy in copies:
+        copy.wait()
+    row_sum = two_levels(esend[1], erecv, 1)[1]
+    copies = node_round(2, row_sum)
+    exchange(back2, ret2, 10, -1, turns[3], nleaf, half)
+    beside.wait()
+    for copy in copies:
+        copy.wait()
+    sums += [vsend[1] + vrecv[1, 1], row_sum, *two_levels(row_sum, erecv, 2)]
 
     sign8 = jnp.where(eight < 4, -1.0, 1.0)
     value = jnp.zeros((8, 384), F32)
@@ -252,17 +314,22 @@
         value = both[:, 0:384] + sign8 * pltpu.roll(both[:, 384:768], 4, 0)
 
     even = iota((ROWS, 384), 0) % 2 == 0
+
+    def store(quarter, values):
+        values = values[0:used].reshape(leaves, 2, 384).astype(BF16)
+        out_ref[0, :, :, 384 * quarter : 384 * quarter + 384] = values
+
     for part in range(2):
         shift = jnp.where(even, value[4 * part : 4 * part + 1], value[4 * part + 1 : 4 * part + 2])
-        out_ref[:, 768 * part : 768 * part + 384] = (top[part] - shift).astype(BF16)
+        store(2 * part, top[part] - shift)
     wait_for(a2a_rs, ret2, 10, 0, nleaf, half)
     rows = ret2[...].astype(F32).reshape(nleaf * 8, 384).astype(BF16)
     for part in range(2):
-        out_ref[:, 768 * part + 384 : 768 * part + 768] = dot(take[part], rows).astype(BF16)
-
-    for g in range(4):
-        wait_for(a2a_ss, send, g, cuts[g], cuts[g + 1], bulk if g < early else whole)
-        if g < early:
+        store(2 * part + 1, dot(take[part], rows))
+
+    for g in range(groups):
+        wait_for(a2a_ss, send, g, cuts[g], cuts[g + 1], bulk if g == 0 else whole)
+        if g == 0:
             wait_for(a2a_ss, send, 4 + g, cuts[g], cuts[g + 1], tail)
         wait_for(a2a_ss, back1, 6 + g, cuts[g], cuts[g + 1], half)
     wait_for(a2a_ss, back2, 10, 0, nleaf, half)
@@ -280,9 +347,9 @@
     sem = pltpu.SemaphoreType.DMA
     vmem = pl.BlockSpec(memory_space=pltpu.VMEM)
     hbm = pl.BlockSpec(memory_space=pl.ANY)
-    out = pl.pallas_call(
+    return pl.pallas_call(
         functools.partial(kernel, (npanel, nleaf, levels, leaves)),
-        out_shape=jax.ShapeDtypeStruct((ROWS, width2), BF16),
+        out_shape=jax.ShapeDtypeStruct(sources.shape, BF16),
         in_specs=[hbm] * 6,
         out_specs=vmem,
         scratch_shapes=[
@@ -307,11 +374,14 @@
             pltpu.VMEM((rounds, 4, 8, 128), F32),
             pltpu.VMEM((rounds, 8, 384), F32),
             pltpu.VMEM((rounds, 4, 8, 384), F32),
+            pltpu.VMEM((4, 8, 384), F32),
+            pltpu.VMEM((3, 8, 384), F32),
+            pltpu.VMEM((4, 4, 8, 384), F32),
             pltpu.VMEM((levels, 384, 768), BF16),
             pltpu.VMEM((2, ROWS, 384), F32),
-            sem((6,)), sem((npanel,)), sem((npanel,)), sem((npanel,)), sem((npanel,)),
+            pltpu.SemaphoreType.REGULAR, sem((6,)), sem((npanel,)), sem((npanel,)), sem((npanel,)), sem((npanel,)),
             sem((11,)), sem((11,)), sem((rounds, 4)), sem((rounds, 4)), sem((rounds, 4)),
-            sem((rounds, 4)),
+            sem((rounds, 4)), sem((4, 4)), sem((4, 4)),
         ],
         compiler_params=pltpu.CompilerParams(
             collective_id=0, has_side_effects=True, vmem_limit_bytes=67043328
@@ -320,7 +390,6 @@
         sources, transmission.transpose(1, 0, 2), media.reshape(1, leaves), sep_code,
         leaf_factors, sep_factors,
     )
-    return out[: leaves * shots].reshape(1, leaves, shots, width2)
 
 
 def solution(mesh):

time: 105 us -> 99.1 us (0.944)
  the two profiles are of different devices: /device:TPU:16 before, /device:TPU:1 now
where the time goes in v3:
time: 99.1 us; the launch traced here: 98.8 us
  Pallas kernels  96.3 us (97%)
  local copies, waits for them, and re-layouts  1.91 us (2%)
    pallas_call x1, Pallas kernels, on_device(): pl.pallas_call(functools.partial(kernel, (npanel, nleaf, levels, leaves))...  96.3 us

profile of v3, /device:TPU:1, one launch (start us, length us, event | category | flops | bytes accessed | tf_op | source)
XLA Modules:
  0.0 98.8 jit_solution(3926277244961693070)
XLA Ops:
  0.7 96.3 %shard_map.64 = bf16[1,52,2,1536]{3,2,1,0:T(2,128)(2,1)} custom-call(bf16[1,52,2,1536]{3,2,1,0:T(2,128)(2,1)} %src_hbm.1, f32[52,1,128]{2,1,0:T(1,128)} %bitcast.2, s32[1,52]{1,0:T(1,128)} %bitcast.3, s32[1,1]{1,0:T(1,128)S(6)} %copy.8.code_hbm, bf16[1,2,768,768]{3,2,1,0:T(8,128)(2,1)} %fac_hbm.1, bf16[2,2,384,384]{3,2,1,0:T(8,128)(2,1)} %sep_hbm.1), custom_call_target="tpu_custom_call" | custom-call | tf_op jit(solution)/shard_map/pallas_call | solution.py:350
  96.9 1.9 %copy.9 = bf16[1,52,2,1536]{3,2,1,0:T(2,128)(2,1)} copy(bf16[1,52,2,1536]{3,2,1,0:T(2,128)(2,1)} %shard_map.64) | data formatting | bytes 638976

commit v4 on v3

--- a/solution.py
+++ b/solution.py
@@ -246,7 +246,8 @@
 
     def both_slots(rows):
         other = jnp.where(eight % 4 < 2, pltpu.roll(rows, 6, 0), pltpu.roll(rows, 2, 0))
-        return rows + other
+        rows = rows + other
+        return jnp.concatenate([rows[0:2], rows[4:6]], axis=0)
 
     for j in range(NY):
         ysend[j] = both_slots(by_row[j])
@@ -305,22 +306,21 @@
         copy.wait()
     sums += [vsend[1] + vrecv[1, 1], row_sum, *two_levels(row_sum, erecv, 2)]
 
-    sign8 = jnp.where(eight < 4, -1.0, 1.0)
-    value = jnp.zeros((8, 384), F32)
+    value = jnp.zeros((4, 384), F32)
     for level in reversed(range(levels)):
         scale = 1.0 / math.sqrt(leaves * 2 ** (level + 1))
         operand = (sums[level] * scale - value).astype(BF16)
         both = dot(operand, chosen[level])
-        value = both[:, 0:384] + sign8 * pltpu.roll(both[:, 384:768], 4, 0)
+        imag = both[:, 384:768]
+        value = both[:, 0:384] + jnp.concatenate([-imag[2:4], imag[0:2]], axis=0)
 
     even = iota((ROWS, 384), 0) % 2 == 0
 
     def store(quarter, values):
-        values = values[0:used].reshape(leaves, 2, 384).astype(BF16)
-        out_ref[0, :, :, 384 * quarter : 384 * quarter + 384] = values
+        out_ref[:, 384 * quarter : 384 * quarter + 384] = values[0:used].astype(BF16)
 
     for part in range(2):
-        shift = jnp.where(even, value[4 * part : 4 * part + 1], value[4 * part + 1 : 4 * part + 2])
+        shift = jnp.where(even, value[2 * part : 2 * part + 1], value[2 * part + 1 : 2 * part + 2])
         store(2 * part, top[part] - shift)
     wait_for(a2a_rs, ret2, 10, 0, nleaf, half)
     rows = ret2[...].astype(F32).reshape(nleaf * 8, 384).astype(BF16)
@@ -347,9 +347,9 @@
     sem = pltpu.SemaphoreType.DMA
     vmem = pl.BlockSpec(memory_space=pltpu.VMEM)
     hbm = pl.BlockSpec(memory_space=pl.ANY)
-    return pl.pallas_call(
+    out = pl.pallas_call(
         functools.partial(kernel, (npanel, nleaf, levels, leaves)),
-        out_shape=jax.ShapeDtypeStruct(sources.shape, BF16),
+        out_shape=jax.ShapeDtypeStruct((leaves * shots, width2), BF16),
         in_specs=[hbm] * 6,
         out_specs=vmem,
         scratch_shapes=[
@@ -372,11 +372,11 @@
             pltpu.VMEM((nleaf, 8, 384), BF16),
             pltpu.VMEM((rounds, 8, 128), F32),
             pltpu.VMEM((rounds, 4, 8, 128), F32),
-            pltpu.VMEM((rounds, 8, 384), F32),
-            pltpu.VMEM((rounds, 4, 8, 384), F32),
-            pltpu.VMEM((4, 8, 384), F32),
-            pltpu.VMEM((3, 8, 384), F32),
-            pltpu.VMEM((4, 4, 8, 384), F32),
+            pltpu.VMEM((rounds, 4, 384), F32),
+            pltpu.VMEM((rounds, 4, 4, 384), F32),
+            pltpu.VMEM((4, 4, 384), F32),
+            pltpu.VMEM((3, 4, 384), F32),
+            pltpu.VMEM((4, 4, 4, 384), F32),
             pltpu.VMEM((levels, 384, 768), BF16),
             pltpu.VMEM((2, ROWS, 384), F32),
             pltpu.SemaphoreType.REGULAR, sem((6,)), sem((npanel,)), sem((npanel,)), sem((npanel,)), sem((npanel,)),
@@ -390,6 +390,7 @@
         sources, transmission.transpose(1, 0, 2), media.reshape(1, leaves), sep_code,
         leaf_factors, sep_factors,
     )
+    return out.reshape(sources.shape)
 
 
 def solution(mesh):

time: 99.1 us -> 97.6 us (0.985)
  Pallas kernels: 96.3 us -> 95 us
    unnamed x1 -> x0, local copies, waits for them, and re-layouts: 1.91 us -> none
    reshape x0 -> x1, local copies, waits for them, and re-layouts: none -> 1.81 us  [on_device(): return out.reshape(sources.shape)]
    pallas_call x1, Pallas kernels: 96.3 us -> 95 us  [on_device(): pl.pallas_call(functools.partial(kernel, (npanel, nleaf, levels, leaves))...]
where the time goes in v4:
time: 97.6 us; the launch traced here: 97.5 us
  Pallas kernels  95 us (97%)
  local copies, waits for them, and re-layouts  1.81 us (2%)
    pallas_call x1, Pallas kernels, on_device(): pl.pallas_call(functools.partial(kernel, (npanel, nleaf, levels, leaves))...  95 us

profile of v4, /device:TPU:1, one launch (start us, length us, event | category | flops | bytes accessed | tf_op | source)
XLA Modules:
  0.0 97.5 jit_solution(14602916862117561685)
XLA Ops:
  0.7 95.0 %shard_map.64 = bf16[104,1536]{1,0:T(8,128)(2,1)} custom-call(bf16[1,52,2,1536]{3,2,1,0:T(2,128)(2,1)} %src_hbm.1, f32[52,1,128]{2,1,0:T(1,128)} %bitcast.2, s32[1,52]{1,0:T(1,128)} %bitcast.3, s32[1,1]{1,0:T(1,128)S(6)} %copy.7.code_hbm, bf16[1,2,768,768]{3,2,1,0:T(8,128)(2,1)} %fac_hbm.1, bf16[2,2,384,384]{3,2,1,0:T(8,128)(2,1)} %sep_hbm.1), custom_call_target="tpu_custom_call" | custom-call | tf_op jit(solution)/shard_map/pallas_call | solution.py:350
  95.7 1.8 %reshape.7 = bf16[1,52,2,1536]{3,2,1,0:T(2,128)(2,1)} reshape(bf16[104,1536]{1,0:T(8,128)(2,1)} %shard_map.64) | data formatting | bytes 638976 | tf_op jit(solution)/shard_map/reshape | solution.py:393
